TPU v7x, 32 devices: a whole 2x2x4 slice. The times are simulated.
32 devices in a mesh: dp: 8 (over z, x), tensor: 4 (over y, core).
Axes of the slice: x: 2, y: 2, z: 4, core: 2. Of those that a mesh axis runs over, the one named last changes fastest.
Arguments:
- hidden_in: float32 [4096, 1536], P('dp'), may hold values from -6 to 6
- doc_lengths: int32 [2, 2], replicated, may hold values from 1 to 1792, 2048 in all within a row
- norm_attn: float32 [2, 1536], replicated, may hold values from 0.5 to 1.5
- norm_mlp: float32 [2, 1536], replicated, may hold values from 0.5 to 1.5
- w_query: bfloat16 [2, 1536, 1536], P(None, None, 'tensor'), may hold values from -0.15625 to 0.15625
- w_key: bfloat16 [2, 1536, 768], P(None, None, 'tensor'), may hold values from -0.15625 to 0.15625
- w_value: bfloat16 [2, 1536, 768], P(None, None, 'tensor'), may hold values from -0.15625 to 0.15625
- w_out: bfloat16 [2, 1536, 1536], P(None, 'tensor'), may hold values from -0.625 to 0.625
- w_gate: bfloat16 [2, 1536, 4096], P(None, None, 'tensor'), may hold values from -0.15625 to 0.15625
- w_up: bfloat16 [2, 1536, 4096], P(None, None, 'tensor'), may hold values from -0.15625 to 0.15625
- w_down: bfloat16 [2, 4096, 1536], P(None, 'tensor'), may hold values from -0.09375 to 0.09375
- cotangent: float32 [4096, 1536], P('dp'), may hold values from -6 to 6
Outputs:
- hidden_out: float32 [4096, 1536], P('dp')
- input_grad: float32 [4096, 1536], P('dp')
- norm_attn_grad: float32 [2, 1536], P(None, 'dp')
- norm_mlp_grad: float32 [2, 1536], P(None, 'dp')
- w_query_grad: float32 [2, 1536, 1536], P(None, 'dp', 'tensor')
- w_key_grad: float32 [2, 1536, 768], P(None, 'dp', 'tensor')
- w_value_grad: float32 [2, 1536, 768], P(None, 'dp', 'tensor')
- w_out_grad: float32 [2, 1536, 1536], P(None, 'tensor', 'dp')
- w_gate_grad: float32 [2, 1536, 4096], P(None, 'dp', 'tensor')
- w_up_grad: float32 [2, 1536, 4096], P(None, 'dp', 'tensor')
- w_down_grad: float32 [2, 4096, 1536], P(None, 'tensor', 'dp')
Inputs may be any that keep to these rules, and one draw needn't show every extreme that they name: `doc_lengths`: each row holds 2 document lengths that add up to 2048, each at most 1792.
All inputs are finite; a program needn't handle non-finite values.
Results may differ from a plain program's by a relative error of at most 0.028.
Values may be sent and summed in bfloat16 or wider, within the bound.
No kernel may reach another device: no remote copies, remote signals or barrier semaphores. Data moves between devices by JAX's collectives and lax.ppermute only.
A program may use at most 320 MiB of HBM per device.

v0:
```python
import jax
import jax.numpy as jnp
from jax import lax
from jax.sharding import PartitionSpec as P

HD = 96
LAYERS = 2
STRETCHES = 4
EPS = 1e-05
BASE = 100000.0


def passed_along(block, axis, distance):
    devices = range(lax.axis_size(axis))
    route = [((i - distance) % len(devices), i) for i in devices]
    return lax.ppermute(block, axis, route)


def rope_tables(positions):
    half_dim = HD // 2
    frequency = BASE ** (-(jnp.arange(half_dim, dtype=jnp.float32) * 2.0 / HD))
    angles = positions.astype(jnp.float32)[:, None] * frequency[None, :]
    angles = jnp.concatenate([angles, angles], axis=1)
    return (jnp.cos(angles)[:, None, :], jnp.sin(angles)[:, None, :])


def rotate(values, cosine, sine_table):
    half_dim = values.shape[-1] // 2
    turned = jnp.concatenate([-values[..., half_dim:], values[..., :half_dim]], axis=-1)
    return values * cosine + turned * sine_table


def unrotate(gradient, cosine, sine_table):
    half_dim = gradient.shape[-1] // 2
    scaled_values = gradient * sine_table
    turned = jnp.concatenate(
        [scaled_values[..., half_dim:], -scaled_values[..., :half_dim]], axis=-1
    )
    return gradient * cosine + turned


def doc_place(places, lengths):
    doc_ends = jnp.cumsum(lengths, axis=1)
    passed = (places[:, None] >= doc_ends).astype(jnp.int32)
    doc_ids = jnp.sum(passed, axis=1)
    starts = jnp.sum(passed * lengths, axis=1)
    return (doc_ids, places - starts)


def scores_of(queries, key_rows, allowed):
    scores = jnp.einsum(
        "qkgd,tkd->kgqt", queries, key_rows, preferred_element_type=jnp.float32
    ) * HD ** (-0.5)
    return jnp.where(allowed[None, None], scores, -jnp.inf)


def attention_forward(queries, key_rows, value_rows, allowed):
    scores = scores_of(queries, key_rows, allowed)
    row_top = jnp.max(scores, axis=-1, keepdims=True)
    log_total = row_top + jnp.log(jnp.sum(jnp.exp(scores - row_top), axis=-1, keepdims=True))
    attn_probs = jnp.exp(scores - log_total).astype(jnp.bfloat16)
    mixed_heads = jnp.einsum(
        "kgqt,tkd->qkgd", attn_probs, value_rows, preferred_element_type=jnp.float32
    )
    return (mixed_heads.astype(jnp.bfloat16), log_total)


def attention_backward(queries, key_rows, value_rows, allowed, log_total, mixed_grad):
    scores = scores_of(queries, key_rows, allowed)
    attn_probs = jnp.exp(scores - log_total)
    prob_grad = jnp.einsum(
        "qkgd,tkd->kgqt", mixed_grad, value_rows, preferred_element_type=jnp.float32
    )
    centre = jnp.sum(attn_probs * prob_grad, axis=-1, keepdims=True)
    score_grad = (attn_probs * (prob_grad - centre) * HD ** (-0.5)).astype(jnp.bfloat16)
    probs_bf = attn_probs.astype(jnp.bfloat16)
    value_grad = jnp.einsum(
        "kgqt,qkgd->tkd", probs_bf, mixed_grad, preferred_element_type=jnp.float32
    )
    query_grad = jnp.einsum(
        "kgqt,tkd->qkgd", score_grad, key_rows, preferred_element_type=jnp.float32
    )
    key_grad = jnp.einsum("kgqt,qkgd->tkd", score_grad, queries, preferred_element_type=jnp.float32)
    return (query_grad, key_grad, value_grad)


def norm_back(residual_stream, inverse_norm, gain, normalized_gradient, incoming_gradient):
    normalized_input = residual_stream * inverse_norm
    scaled_values = normalized_gradient * gain
    gain_gradient = jnp.sum(normalized_gradient * normalized_input, axis=0)
    residual_gradient = incoming_gradient + inverse_norm * (
        scaled_values
        - normalized_input * jnp.mean(scaled_values * normalized_input, axis=1, keepdims=True)
    )
    return (residual_gradient, gain_gradient)


def forward_layer(residual_stream, params, tables, allowed):
    gain_attn, gain_mlp, query_w, key_w, value_w, out_w, gate_w, up_w, down_w = params
    cosine, sine_table = tables
    row_count = residual_stream.shape[0]
    query_heads = query_w.shape[1] // HD
    kv_heads = key_w.shape[1] // HD
    inv_attn = lax.rsqrt(jnp.mean(residual_stream * residual_stream, axis=1, keepdims=True) + EPS)
    normed_attn = (residual_stream * inv_attn * gain_attn).astype(jnp.bfloat16)
    queries = jnp.dot(normed_attn, query_w, preferred_element_type=jnp.float32).reshape(
        row_count, query_heads, HD
    )
    queries = rotate(queries, cosine, sine_table).astype(jnp.bfloat16)
    key_rows = jnp.dot(normed_attn, key_w, preferred_element_type=jnp.float32).reshape(
        row_count, kv_heads, HD
    )
    key_rows = (
        rotate(key_rows, cosine, sine_table).astype(jnp.bfloat16).reshape(row_count, kv_heads * HD)
    )
    value_rows = jnp.dot(normed_attn, value_w, preferred_element_type=jnp.float32).astype(
        jnp.bfloat16
    )
    key_list = [key_rows]
    value_list = [value_rows]
    for distance in range(1, STRETCHES):
        moved_keys, moved_values = passed_along((key_rows, value_rows), "dp", distance)
        key_list.append(moved_keys)
        value_list.append(moved_values)
    all_keys = jnp.concatenate(key_list, axis=0).reshape(STRETCHES * row_count, kv_heads, HD)
    all_values = jnp.concatenate(value_list, axis=0).reshape(STRETCHES * row_count, kv_heads, HD)
    grouped = queries.reshape(row_count, kv_heads, query_heads // kv_heads, HD)
    mixed_heads, log_total = attention_forward(grouped, all_keys, all_values, allowed)
    mixed_heads = mixed_heads.reshape(row_count, query_heads * HD)
    head_part = jnp.dot(mixed_heads, out_w, preferred_element_type=jnp.float32)
    middle = residual_stream + lax.psum(head_part, "tensor")
    inv_mlp = lax.rsqrt(jnp.mean(middle * middle, axis=1, keepdims=True) + EPS)
    normed_mlp = (middle * inv_mlp * gain_mlp).astype(jnp.bfloat16)
    gate_pre = jnp.dot(normed_mlp, gate_w, preferred_element_type=jnp.float32)
    up_values = jnp.dot(normed_mlp, up_w, preferred_element_type=jnp.float32)
    activated = (jax.nn.silu(gate_pre) * up_values).astype(jnp.bfloat16)
    unit_part = jnp.dot(activated, down_w, preferred_element_type=jnp.float32)
    result = middle + lax.psum(unit_part, "tensor")
    record = (
        residual_stream,
        inv_attn,
        normed_attn,
        grouped,
        all_keys,
        all_values,
        log_total,
        mixed_heads,
        middle,
        inv_mlp,
        normed_mlp,
        gate_pre,
        up_values,
        activated,
    )
    return (record, result)


def backward_layer(grad_flow, record, params, tables, allowed):
    gain_attn, gain_mlp, query_w, key_w, value_w, out_w, gate_w, up_w, down_w = params
    (
        residual_stream,
        inv_attn,
        normed_attn,
        grouped,
        all_keys,
        all_values,
        log_total,
        mixed_heads,
        middle,
        inv_mlp,
        normed_mlp,
        gate_pre,
        up_values,
        activated,
    ) = record
    cosine, sine_table = tables
    row_count = residual_stream.shape[0]
    query_heads = query_w.shape[1] // HD
    kv_heads = key_w.shape[1] // HD
    down_in = grad_flow.astype(jnp.bfloat16)
    grad_down = jnp.dot(activated.T, down_in, preferred_element_type=jnp.float32)
    hidden_grad = jnp.dot(down_in, down_w.T, preferred_element_type=jnp.float32)
    sigmoid_gate = jax.nn.sigmoid(gate_pre)
    gate_grad = (
        hidden_grad * up_values * sigmoid_gate * (1.0 + gate_pre * (1.0 - sigmoid_gate))
    ).astype(jnp.bfloat16)
    up_grad = (hidden_grad * gate_pre * sigmoid_gate).astype(jnp.bfloat16)
    grad_gate = jnp.dot(normed_mlp.T, gate_grad, preferred_element_type=jnp.float32)
    grad_up = jnp.dot(normed_mlp.T, up_grad, preferred_element_type=jnp.float32)
    unit_back = jnp.dot(gate_grad, gate_w.T, preferred_element_type=jnp.float32) + jnp.dot(
        up_grad, up_w.T, preferred_element_type=jnp.float32
    )
    mlp_norm_grad = lax.psum(unit_back, "tensor")
    middle_grad, grad_gain_mlp = norm_back(middle, inv_mlp, gain_mlp, mlp_norm_grad, grad_flow)
    out_in = middle_grad.astype(jnp.bfloat16)
    grad_out = jnp.dot(mixed_heads.T, out_in, preferred_element_type=jnp.float32)
    mixed_grad = jnp.dot(out_in, out_w.T, preferred_element_type=jnp.float32).astype(jnp.bfloat16)
    mixed_grad = mixed_grad.reshape(row_count, kv_heads, query_heads // kv_heads, HD)
    query_grad, key_grad, value_grad = attention_backward(
        grouped, all_keys, all_values, allowed, log_total, mixed_grad
    )
    key_grad = key_grad.reshape(STRETCHES * row_count, kv_heads * HD)
    value_grad = value_grad.reshape(STRETCHES * row_count, kv_heads * HD)
    key_total = key_grad[:row_count]
    value_total = value_grad[:row_count]
    for distance in range(1, STRETCHES):
        key_piece = key_grad[distance * row_count : (distance + 1) * row_count]
        value_piece = value_grad[distance * row_count : (distance + 1) * row_count]
        moved_keys, moved_values = passed_along((key_piece, value_piece), "dp", -distance)
        key_total = key_total + moved_keys
        value_total = value_total + moved_values
    query_grad = (
        unrotate(query_grad.reshape(row_count, query_heads, HD), cosine, sine_table)
        .astype(jnp.bfloat16)
        .reshape(row_count, query_heads * HD)
    )
    key_total = (
        unrotate(key_total.reshape(row_count, kv_heads, HD), cosine, sine_table)
        .astype(jnp.bfloat16)
        .reshape(row_count, kv_heads * HD)
    )
    value_total = value_total.astype(jnp.bfloat16)
    grad_query = jnp.dot(normed_attn.T, query_grad, preferred_element_type=jnp.float32)
    grad_key = jnp.dot(normed_attn.T, key_total, preferred_element_type=jnp.float32)
    grad_value = jnp.dot(normed_attn.T, value_total, preferred_element_type=jnp.float32)
    head_back = jnp.dot(query_grad, query_w.T, preferred_element_type=jnp.float32)
    head_back = head_back + jnp.dot(key_total, key_w.T, preferred_element_type=jnp.float32)
    head_back = head_back + jnp.dot(value_total, value_w.T, preferred_element_type=jnp.float32)
    attn_norm_grad = lax.psum(head_back, "tensor")
    residual_gradient, grad_gain_attn = norm_back(
        residual_stream, inv_attn, gain_attn, attn_norm_grad, middle_grad
    )
    return (
        residual_gradient,
        (
            grad_gain_attn,
            grad_gain_mlp,
            grad_query,
            grad_key,
            grad_value,
            grad_out,
            grad_gate,
            grad_up,
            grad_down,
        ),
    )


def shards(
    hidden_in,
    doc_lengths,
    norm_attn,
    norm_mlp,
    w_query,
    w_key,
    w_value,
    w_out,
    w_gate,
    w_up,
    w_down,
    cotangent,
):
    row_count = hidden_in.shape[0]
    seq_count = lax.axis_size("dp") // STRETCHES
    shifted_index = lax.axis_index("dp") + STRETCHES // 2
    stretch_index = shifted_index % STRETCHES
    seq_index = shifted_index // STRETCHES % seq_count
    lengths = lax.dynamic_slice_in_dim(doc_lengths, seq_index, 1, 0)
    local_rows = jnp.arange(row_count, dtype=jnp.int32)
    query_place = stretch_index * row_count + local_rows
    query_doc, query_pos = doc_place(query_place, lengths)
    key_parts = []
    for distance in range(STRETCHES):
        key_parts.append((stretch_index - distance) * row_count + local_rows)
    key_place = jnp.concatenate(key_parts)
    key_doc = doc_place(key_place, lengths)[0]
    allowed = (
        (key_place[None, :] >= 0)
        & (key_place[None, :] <= query_place[:, None])
        & (key_doc[None, :] == query_doc[:, None])
    )
    tables = rope_tables(query_pos)
    records = []
    flowing = hidden_in
    for layer_index in range(LAYERS):
        params = (
            norm_attn[layer_index],
            norm_mlp[layer_index],
            w_query[layer_index],
            w_key[layer_index],
            w_value[layer_index],
            w_out[layer_index],
            w_gate[layer_index],
            w_up[layer_index],
            w_down[layer_index],
        )
        record, flowing = forward_layer(flowing, params, tables, allowed)
        records.append(record)
    grad_flow = cotangent
    collected = [None] * LAYERS
    for layer_index in reversed(range(LAYERS)):
        params = (
            norm_attn[layer_index],
            norm_mlp[layer_index],
            w_query[layer_index],
            w_key[layer_index],
            w_value[layer_index],
            w_out[layer_index],
            w_gate[layer_index],
            w_up[layer_index],
            w_down[layer_index],
        )
        grad_flow, layer_grads = backward_layer(
            grad_flow, records[layer_index], params, tables, allowed
        )
        collected[layer_index] = layer_grads
    stacked = tuple(
        (jnp.stack([member[position] for member in collected]) for position in range(9))
    )
    stacked = (
        lax.psum_scatter(
            stacked[0].astype(jnp.bfloat16), "dp", scatter_dimension=1, tiled=True
        ).astype(jnp.float32),
        lax.psum_scatter(
            stacked[1].astype(jnp.bfloat16), "dp", scatter_dimension=1, tiled=True
        ).astype(jnp.float32),
        lax.psum_scatter(
            stacked[2].astype(jnp.bfloat16), "dp", scatter_dimension=1, tiled=True
        ).astype(jnp.float32),
        lax.psum_scatter(
            stacked[3].astype(jnp.bfloat16), "dp", scatter_dimension=1, tiled=True
        ).astype(jnp.float32),
        lax.psum_scatter(
            stacked[4].astype(jnp.bfloat16), "dp", scatter_dimension=1, tiled=True
        ).astype(jnp.float32),
        lax.psum_scatter(
            stacked[5].astype(jnp.bfloat16), "dp", scatter_dimension=2, tiled=True
        ).astype(jnp.float32),
        lax.psum_scatter(
            stacked[6].astype(jnp.bfloat16), "dp", scatter_dimension=1, tiled=True
        ).astype(jnp.float32),
        lax.psum_scatter(
            stacked[7].astype(jnp.bfloat16), "dp", scatter_dimension=1, tiled=True
        ).astype(jnp.float32),
        lax.psum_scatter(
            stacked[8].astype(jnp.bfloat16), "dp", scatter_dimension=2, tiled=True
        ).astype(jnp.float32),
    )
    return (
        flowing,
        grad_flow,
        stacked[0],
        stacked[1],
        stacked[2],
        stacked[3],
        stacked[4],
        stacked[5],
        stacked[6],
        stacked[7],
        stacked[8],
    )


def solution(mesh):
    placed = (
        P("dp", None),
        P(),
        P(),
        P(),
        P(None, None, "tensor"),
        P(None, None, "tensor"),
        P(None, None, "tensor"),
        P(None, "tensor", None),
        P(None, None, "tensor"),
        P(None, None, "tensor"),
        P(None, "tensor", None),
        P("dp", None),
    )
    return jax.shard_map(
        shards,
        mesh=mesh,
        in_specs=placed,
        out_specs=(
            P("dp", None),
            P("dp", None),
            P(None, "dp"),
            P(None, "dp"),
            P(None, "dp", "tensor"),
            P(None, "dp", "tensor"),
            P(None, "dp", "tensor"),
            P(None, "tensor", "dp"),
            P(None, "dp", "tensor"),
            P(None, "dp", "tensor"),
            P(None, "tensor", "dp"),
        ),
        check_vma=False,
    )
```

profile of v0, /device:TPU:0, one launch (start us, length us, event | category | flops | bytes accessed | tf_op | source)
XLA Modules:
  0.0 1885.0 jit_solution(11726850413629536480)
XLA Ops:
  38.5 14.9 collective-permute-done.5
  53.4 4.6 fusion.10
  58.0 3.6 exponential_reduce_fusion.1
  63.8 4.4 convolution_convert_fusion.15
  72.2 64.6 %all-reduce.13.cloned.1.call-done = f32[512,1536]{1,0:T(8,128)} async-done(((f32[512,1536]{1,0:T(8,128)}), f32[512,1536]{1,0:T(8,128)}) %all-reduce.13.cloned.1.call-update) | async-done | bytes 3145744 | tf_op jit(solution)/shard_map/psum | solution.py:131
  140.5 4.5 fusion.38
  145.1 3.3 multiply_convert_fusion.9
  149.4 3.5 fusion.31
  155.3 66.3 %all-reduce.15.cloned.1.call-done = f32[512,1536]{1,0:T(8,128)} async-done(((f32[512,1536]{1,0:T(8,128)}), f32[512,1536]{1,0:T(8,128)}) %all-reduce.15.cloned.1.call-update) | async-done | bytes 3145744 | tf_op jit(solution)/shard_map/psum | solution.py:138
  238.2 22.7 %collective-permute-done.11 = bf16[512,192]{0,1:T(8,128)(2,1)S(1)} collective-permute-done((bf16[512,192]{0,1:T(8,128)(2,1)S(1)}, bf16[512,192]{0,1:T(8,128)(2,1)S(1)}, u32[]{:S(2)}, u32[]{:S(2)}) %collective-permute-start.11) | collective-permute-done | bytes 196640 | tf_op jit(solution)/shard_map/ppermute | solution.py:16
  264.0 3.6 exponential_reduce_fusion
  269.7 4.4 convolution_convert_fusion.14
  274.9 3.9 fusion.77
  279.3 64.6 %all-reduce.17.cloned.1.call-done = f32[512,1536]{1,0:T(8,128)} async-done(((f32[512,1536]{1,0:T(8,128)}), f32[512,1536]{1,0:T(8,128)}) %all-reduce.17.cloned.1.call-update) | async-done | bytes 3145744 | tf_op jit(solution)/shard_map/psum | solution.py:131
  347.7 5.6 fusion.23
  356.0 3.6 multiply_convert_fusion.6
  361.5 3.5 convolution_add_fusion.5
  365.1 68.7 %all-reduce.19.cloned.1.call-done = f32[512,1536]{1,0:T(8,128)} async-done(((f32[512,1536]{1,0:T(8,128)}), f32[512,1536]{1,0:T(8,128)}) %all-reduce.19.cloned.1.call-update) | async-done | bytes 3145744 | tf_op jit(solution)/shard_map/psum | solution.py:193
  433.7 4.3 multiply_reduce_fusion
  444.3 9.5 convolution_bitcast_fusion.1
  453.8 8.2 fusion.188
  462.0 25.3 %fusion.63 = f32[2048,2,96]{0,2,1:T(8,128)} fusion(bf16[512,2,2,96]{0,3,2,1:T(8,128)(2,1)} %bitcast.491, f32[2,2048,512,2]{2,1,3,0:T(8,128)} %fusion.188, f32[2,2048,512,2]{2,1,3,0:T(8,128)} %copy-done.12, f32[2,2,512]{2,1,0:T(2,128)} %copy-done.94, pred[512,2048]{0,1:T(8,128)(4,1)} %copy-done.25), kind=kOutput, calls=%fused_computation.113 | convolution fusion | flops 851447808 | bytes 36577280 | tf_op jit(solution)/shard_map/kgqt,qkgd->tkd/dot_general | solution.py:83
  487.3 25.1 %fusion.41 = f32[2,96,2,512]{3,1,2,0:T(8,128)} fusion(f32[2,2048,512,2]{2,1,3,0:T(8,128)} %fusion.188, f32[2,2048,512,2]{2,1,3,0:T(8,128)} %copy-done.12, f32[2,2,512]{2,1,0:T(2,128)} %copy-done.94, pred[512,2048]{0,1:T(8,128)(4,1)} %copy-done.25, bf16[512,2,96]{0,2,1:T(8,128)(2,1)} %bitcast.530, bf16[512,2,96]{0,2,1:T(8,128)(2,1)} %bitcast.528, ...), kind=kOutput, calls=%fused_computation.87 | convolution fusion | flops 854593536 | bytes 36184064 | tf_op jit(solution)/shard_map/kgqt,tkd->qkgd/dot_general | solution.py:80
  514.0 4.3 collective-permute-start.15
  520.2 3.3 collective-permute-start.14
  525.8 19.0 %collective-permute-done.12 = f32[512,192]{0,1:T(8,128)S(1)} collective-permute-done((f32[512,192]{0,1:T(8,128)S(1)}, f32[512,192]{0,1:T(8,128)S(1)}, u32[]{:S(2)}, u32[]{:S(2)}) %collective-permute-start.12) | collective-permute-done | bytes 393248 | tf_op jit(solution)/shard_map/ppermute | solution.py:16
  547.4 5.8 collective-permute-done.13
  553.2 8.4 collective-permute-done.14
  562.7 6.1 collective-permute-done.17
  571.9 86.6 %all-reduce.21.cloned.1.call-done = f32[512,1536]{1,0:T(8,128)} async-done(((f32[512,1536]{1,0:T(8,128)}), f32[512,1536]{1,0:T(8,128)}) %all-reduce.21.cloned.1.call-update) | async-done | bytes 3145744 | tf_op jit(solution)/shard_map/psum | solution.py:229
  658.6 4.3 multiply_reduce_fusion.2
  666.2 6.6 multiply_convert_fusion.4
  674.8 3.6 convolution_add_fusion.4
  678.5 5.7 fusion.20
  684.1 63.0 %all-reduce.23.cloned.1.call-done = f32[512,1536]{1,0:T(8,128)} async-done(((f32[512,1536]{1,0:T(8,128)}), f32[512,1536]{1,0:T(8,128)}) %all-reduce.23.cloned.1.call-update) | async-done | bytes 3145744 | tf_op jit(solution)/shard_map/psum | solution.py:193
  754.7 9.7 convolution_bitcast_fusion
  764.4 8.1 fusion.189
  772.5 24.6 %fusion.62 = f32[2048,2,96]{0,2,1:T(8,128)} fusion(bf16[512,2,2,96]{0,3,2,1:T(8,128)(2,1)S(1)} %bitcast.489, f32[2,2048,512,2]{2,1,3,0:T(8,128)} %fusion.189, f32[2,2048,512,2]{2,1,3,0:T(8,128)} %copy-done.11, f32[2,2,512]{2,1,0:T(2,128)S(1)} %copy-done.93, pred[512,2048]{0,1:T(8,128)(4,1)S(1)} %copy-done.28), kind=kOutput, calls=%fused_computation.112 | convolution fusion | flops 851447808 | bytes 36577280 | tf_op jit(solution)/shard_map/kgqt,qkgd->tkd/dot_general | solution.py:83
  797.2 23.6 %fusion.44 = f32[2,96,2,512]{3,1,2,0:T(8,128)S(1)} fusion(f32[2,2048,512,2]{2,1,3,0:T(8,128)} %fusion.189, f32[2,2048,512,2]{2,1,3,0:T(8,128)} %copy-done.11, f32[2,2,512]{2,1,0:T(2,128)S(1)} %copy-done.93, pred[512,2048]{0,1:T(8,128)(4,1)S(1)} %copy-done.28, bf16[512,2,96]{0,2,1:T(8,128)(2,1)} %bitcast.14, bf16[512,2,96]{0,2,1:T(8,128)(2,1)} %bitcast.13, ...), kind=kOutput, calls=%fused_computation.90 | convolution fusion | flops 854593536 | bytes 36184064 | tf_op jit(solution)/shard_map/kgqt,tkd->qkgd/dot_general | solution.py:80
  822.6 4.3 collective-permute-start.21
  828.8 3.3 collective-permute-start.20
  834.4 19.0 %collective-permute-done.18 = f32[512,192]{0,1:T(8,128)S(1)} collective-permute-done((f32[512,192]{0,1:T(8,128)S(1)}, f32[512,192]{0,1:T(8,128)S(1)}, u32[]{:S(2)}, u32[]{:S(2)}) %collective-permute-start.18) | collective-permute-done | bytes 393248 | tf_op jit(solution)/shard_map/ppermute | solution.py:16
  855.9 5.9 collective-permute-done.19
  861.8 8.4 collective-permute-done.20
  871.3 6.1 collective-permute-done.23
  887.9 4.9 copy.91
  892.7 4.5 reshape.440
  900.3 3.7 copy.89
  907.7 3.6 fusion.58
  913.4 105.2 %all-reduce.25.cloned.1.call-done = (f32[512,1536]{1,0:T(8,128)}, f32[512,1536]{1,0:T(8,128)}) async-done(((f32[512,1536]{1,0:T(8,128)}, f32[512,1536]{1,0:T(8,128)}), (f32[512,1536]{1,0:T(8,128)}, f32[512,1536]{1,0:T(8,128)})) %all-reduce.25.cloned.1.call-update) | async-done | bytes 6291472 | tf_op jit(solution)/shard_map/psum | solution.py:138
  1022.3 3.3 pad_maximum_fusion.3
  1025.9 4.2 fusion.17
  1037.8 16.4 copy.64
  1058.7 6.8 copy.63
  1065.6 3.7 fusion.15
  1074.6 3.7 fusion.13
  1086.7 63.9 %reduce-scatter.28.cloned.1.call-done = bf16[192,384]{1,0:T(8,128)(2,1)} async-done(((bf16[1536,384]{1,0:T(8,128)(2,1)}), bf16[192,384]{1,0:T(8,128)(2,1)}) %reduce-scatter.28.cloned.1.call-update) | async-done | bytes 147472
  1152.8 64.8 %reduce-scatter.26.cloned.1.call-done = bf16[192,384]{1,0:T(8,128)(2,1)} async-done(((bf16[1536,384]{1,0:T(8,128)(2,1)}), bf16[192,384]{1,0:T(8,128)(2,1)}) %reduce-scatter.26.cloned.1.call-update) | async-done | bytes 147472
  1219.7 5.2 add.306
  1227.4 54.4 %reduce-scatter.22.cloned.1.call-done = bf16[192,2]{1,0:T(8,128)(2,1)} async-done(((bf16[1536,2]{1,0:T(8,128)(2,1)}), bf16[192,2]{1,0:T(8,128)(2,1)}) %reduce-scatter.22.cloned.1.call-update) | async-done | bytes 784
  1283.3 69.9 %reduce-scatter.16.cloned.1.call-done = bf16[2,192,384]{2,1,0:T(8,128)(2,1)} async-done(((bf16[2,1536,384]{2,1,0:T(8,128)(2,1)}), bf16[2,192,384]{2,1,0:T(8,128)(2,1)}) %reduce-scatter.16.cloned.1.call-update) | async-done | bytes 294928 | tf_op jit(solution)/shard_map/reduce_scatter | solution.py:327
  1355.0 278.8 %all-reduce.27.cloned.1.call-done = (bf16[2,384,1536]{1,0,2:T(2,128)(2,1)}, bf16[2,1024,1536]{1,0,2:T(2,128)(2,1)}) async-done(((bf16[2,384,1536]{1,0,2:T(2,128)(2,1)}, bf16[2,1024,1536]{1,0,2:T(2,128)(2,1)}), (bf16[2,384,1536]{1,0,2:T(2,128)(2,1)}, bf16[2,1024,1536]{1,0,2:T(2,128)(2,1)})) %all-reduce.27.cloned.1.call-update) | async-done | bytes 8650768
  1639.1 115.5 %reduce-scatter.20.cloned.1.call-done = bf16[2,192,1024]{2,1,0:T(8,128)(2,1)} async-done(((bf16[2,1536,1024]{2,1,0:T(8,128)(2,1)}), bf16[2,192,1024]{2,1,0:T(8,128)(2,1)}) %reduce-scatter.20.cloned.1.call-update) | async-done | bytes 786448 | tf_op jit(solution)/shard_map/reduce_scatter | solution.py:342
  1757.1 118.5 %reduce-scatter.18.cloned.1.call-done = bf16[2,192,1024]{2,1,0:T(8,128)(2,1)} async-done(((bf16[2,1536,1024]{2,1,0:T(8,128)(2,1)}), bf16[2,192,1024]{2,1,0:T(8,128)(2,1)}) %reduce-scatter.18.cloned.1.call-update) | async-done | bytes 786448 | tf_op jit(solution)/shard_map/reduce_scatter | solution.py:339
  (463 shorter events, 184.6 us)
Async XLA Ops:
  7.2 129.6 %all-reduce.13.cloned.1.call-start = ((), (), s32[]{:S(2)}) async-start(), calls=%async_computation.7 | async-start | bytes 6291456 | tf_op jit(solution)/shard_map/psum | solution.py:131
  15.3 9.3 copy-start.13
  15.9 10.4 copy-start.77
  16.8 19.0 %collective-permute-start.3 = (bf16[512,192]{0,1:T(8,128)(2,1)}, bf16[512,192]{0,1:T(8,128)(2,1)}, u32[]{:S(2)}, u32[]{:S(2)}) collective-permute-start(bf16[512,192]{0,1:T(8,128)(2,1)} %bitcast.11), channel_id=1, source_target_pairs={{28,0},{0,4},{4,8},{8,12},{12,16},{16,20},{20,24},{24,28},{29,1},{... | collective-permute-start | bytes 589832 | tf_op jit(solution)/shard_map/ppermute | solution.py:16
  19.7 18.7 collective-permute-start.4
  21.3 32.1 %collective-permute-start.5 = (bf16[512,192]{0,1:T(8,128)(2,1)}, bf16[512,192]{0,1:T(8,128)(2,1)}, u32[]{:S(2)}, u32[]{:S(2)}) collective-permute-start(bf16[512,192]{0,1:T(8,128)(2,1)} %bitcast.11), channel_id=1, source_target_pairs={{20,0},{24,4},{28,8},{0,12},{4,16},{8,20},{12,24},{16,28},{21,1},{... | collective-permute-start | bytes 589832 | tf_op jit(solution)/shard_map/ppermute | solution.py:16
  24.6 37.1 %collective-permute-start = (bf16[512,192]{0,1:T(8,128)(2,1)S(1)}, bf16[512,192]{0,1:T(8,128)(2,1)S(1)}, u32[]{:S(2)}, u32[]{:S(2)}) collective-permute-start(bf16[512,192]{0,1:T(8,128)(2,1)S(1)} %convolution_convert_fusion.19), channel_id=1, source_target_pairs={{28,0},{0,4},{4,8},{8,12},{12,16},{16,20},{20,24},{24,28},{29,1},{... | collective-permute-start | bytes 589832 | tf_op jit(solution)/shard_map/ppermute | solution.py:16
  26.1 35.6 %collective-permute-start.1 = (bf16[512,192]{0,1:T(8,128)(2,1)S(1)}, bf16[512,192]{0,1:T(8,128)(2,1)}, u32[]{:S(2)}, u32[]{:S(2)}) collective-permute-start(bf16[512,192]{0,1:T(8,128)(2,1)S(1)} %convolution_convert_fusion.19), channel_id=1, source_target_pairs={{24,0},{28,4},{0,8},{4,12},{8,16},{12,20},{16,24},{20,28},{25,1},{... | collective-permute-start | bytes 589832 | tf_op jit(solution)/shard_map/ppermute | solution.py:16
  35.6 27.4 %copy-start.25 = (pred[512,2048]{0,1:T(8,128)(4,1)}, pred[512,2048]{0,1:T(8,128)(4,1)S(1)}, u32[]{:S(2)}) copy-start(pred[512,2048]{0,1:T(8,128)(4,1)S(1)} %compare_and_fusion) | copy-start | bytes 3145732
  35.8 22.2 %copy-start.68 = (bf16[512,4,96]{0,2,1:T(8,128)(2,1)}, bf16[512,4,96]{0,2,1:T(8,128)(2,1)S(1)}, u32[]{:S(2)}) copy-start(bf16[512,4,96]{0,2,1:T(8,128)(2,1)S(1)} %fusion.97) | copy-start | bytes 1179652
  35.8 25.9 %collective-permute-start.2 = (bf16[512,192]{0,1:T(8,128)(2,1)S(1)}, bf16[512,192]{0,1:T(8,128)(2,1)S(1)}, u32[]{:S(2)}, u32[]{:S(2)}) collective-permute-start(bf16[512,192]{0,1:T(8,128)(2,1)S(1)} %convolution_convert_fusion.19), channel_id=1, source_target_pairs={{20,0},{24,4},{28,8},{0,12},{4,16},{8,20},{12,24},{16,28},{21,1},{... | collective-permute-start | bytes 589832 | tf_op jit(solution)/shard_map/ppermute | solution.py:16
  70.9 150.6 %all-reduce.15.cloned.1.call-start = ((), (), s32[]{:S(2)}) async-start(), calls=%async_computation.8 | async-start | bytes 6291456 | tf_op jit(solution)/shard_map/psum | solution.py:138
  140.5 8.9 slice-start.10
  152.9 191.1 %all-reduce.17.cloned.1.call-start = ((), (), s32[]{:S(2)}) async-start(), calls=%async_computation.9 | async-start | bytes 6291456 | tf_op jit(solution)/shard_map/psum | solution.py:131
  224.2 10.1 copy-start.16
  226.2 34.7 %copy-start.71 = (bf16[512,2,96]{0,2,1:T(8,128)(2,1)}, bf16[512,2,96]{0,2,1:T(8,128)(2,1)S(1)}, u32[]{:S(2)}) copy-start(bf16[512,2,96]{0,2,1:T(8,128)(2,1)S(1)} %fusion.129) | copy-start | bytes 589828
  226.2 10.7 collective-permute-start.9
  227.8 10.5 collective-permute-start.10
  229.2 31.6 %collective-permute-start.11 = (bf16[512,192]{0,1:T(8,128)(2,1)S(1)}, bf16[512,192]{0,1:T(8,128)(2,1)S(1)}, u32[]{:S(2)}, u32[]{:S(2)}) collective-permute-start(bf16[512,192]{0,1:T(8,128)(2,1)S(1)} %bitcast.506), channel_id=1, source_target_pairs={{20,0},{24,4},{28,8},{0,12},{4,16},{8,20},{12,24},{16,28},{21,1},{... | collective-permute-start | bytes 589832 | tf_op jit(solution)/shard_map/ppermute | solution.py:16
  232.3 35.3 %collective-permute-start.6 = (bf16[512,192]{0,1:T(8,128)(2,1)S(1)}, bf16[512,192]{0,1:T(8,128)(2,1)S(1)}, u32[]{:S(2)}, u32[]{:S(2)}) collective-permute-start(bf16[512,192]{0,1:T(8,128)(2,1)S(1)} %convolution_convert_fusion.18), channel_id=1, source_target_pairs={{28,0},{0,4},{4,8},{8,12},{12,16},{16,20},{20,24},{24,28},{29,1},{... | collective-permute-start | bytes 589832 | tf_op jit(solution)/shard_map/ppermute | solution.py:16
  233.8 33.8 %collective-permute-start.7 = (bf16[512,192]{0,1:T(8,128)(2,1)S(1)}, bf16[512,192]{0,1:T(8,128)(2,1)S(1)}, u32[]{:S(2)}, u32[]{:S(2)}) collective-permute-start(bf16[512,192]{0,1:T(8,128)(2,1)S(1)} %convolution_convert_fusion.18), channel_id=1, source_target_pairs={{24,0},{28,4},{0,8},{4,12},{8,16},{12,20},{16,24},{20,28},{25,1},{... | collective-permute-start | bytes 589832 | tf_op jit(solution)/shard_map/ppermute | solution.py:16
  235.1 25.8 %copy-start.26 = (pred[512,2048]{0,1:T(8,128)(4,1)S(1)}, pred[512,2048]{0,1:T(8,128)(4,1)}, u32[]{:S(2)}) copy-start(pred[512,2048]{0,1:T(8,128)(4,1)} %copy-done.25) | copy-start | bytes 3145732
  235.5 28.4 %copy-start.70 = (bf16[512,4,96]{0,2,1:T(8,128)(2,1)}, bf16[512,4,96]{0,2,1:T(8,128)(2,1)S(1)}, u32[]{:S(2)}) copy-start(bf16[512,4,96]{0,2,1:T(8,128)(2,1)S(1)} %fusion.99) | copy-start | bytes 1179652
  236.9 27.0 %copy-start.98 = (bf16[512,192]{0,1:T(8,128)(2,1)}, bf16[512,192]{0,1:T(8,128)(2,1)S(1)}, u32[]{:S(2)}) copy-start(bf16[512,192]{0,1:T(8,128)(2,1)S(1)} %collective-permute-done.9) | copy-start | bytes 589828
  236.9 30.8 %collective-permute-start.8 = (bf16[512,192]{0,1:T(8,128)(2,1)S(1)}, bf16[512,192]{0,1:T(8,128)(2,1)S(1)}, u32[]{:S(2)}, u32[]{:S(2)}) collective-permute-start(bf16[512,192]{0,1:T(8,128)(2,1)S(1)} %convolution_convert_fusion.18), channel_id=1, source_target_pairs={{20,0},{24,4},{28,8},{0,12},{4,16},{8,20},{12,24},{16,28},{21,1},{... | collective-permute-start | bytes 589832 | tf_op jit(solution)/shard_map/ppermute | solution.py:16
  238.2 25.7 %copy-start.99 = (bf16[512,192]{0,1:T(8,128)(2,1)}, bf16[512,192]{0,1:T(8,128)(2,1)S(1)}, u32[]{:S(2)}) copy-start(bf16[512,192]{0,1:T(8,128)(2,1)S(1)} %collective-permute-done.10) | copy-start | bytes 589828
  278.8 154.9 %all-reduce.19.cloned.1.call-start = ((), (), s32[]{:S(2)}) async-start(), calls=%async_computation.10 | async-start | bytes 6291456 | tf_op jit(solution)/shard_map/psum | solution.py:193
  365.0 293.5 %all-reduce.21.cloned.1.call-start = ((), (), s32[]{:S(2)}) async-start(), calls=%async_computation.11 | async-start | bytes 6291456 | tf_op jit(solution)/shard_map/psum | solution.py:229
  444.3 9.5 copy-start.44
  512.4 11.1 copy-start.34
  514.0 48.6 %collective-permute-start.15 = (f32[512,192]{0,1:T(8,128)S(1)}, f32[512,192]{0,1:T(8,128)S(1)}, u32[]{:S(2)}, u32[]{:S(2)}) collective-permute-start(f32[512,192]{0,1:T(8,128)S(1)} %bitcast.497), channel_id=1, source_target_pairs={{4,0},{8,4},{12,8},{16,12},{20,16},{24,20},{28,24},{0,28},{5,1},{9... | collective-permute-start | bytes 1179656 | tf_op jit(solution)/shard_map/ppermute | solution.py:16
  518.3 44.4 %collective-permute-start.16 = (f32[512,192]{0,1:T(8,128)S(1)}, f32[512,192]{0,1:T(8,128)S(1)}, u32[]{:S(2)}, u32[]{:S(2)}) collective-permute-start(f32[512,192]{0,1:T(8,128)S(1)} %bitcast.495), channel_id=1, source_target_pairs={{8,0},{12,4},{16,8},{20,12},{24,16},{28,20},{0,24},{4,28},{9,1},{1... | collective-permute-start | bytes 1179656 | tf_op jit(solution)/shard_map/ppermute | solution.py:16
  519.0 25.7 %collective-permute-start.12 = (f32[512,192]{0,1:T(8,128)S(1)}, f32[512,192]{0,1:T(8,128)S(1)}, u32[]{:S(2)}, u32[]{:S(2)}) collective-permute-start(f32[512,192]{0,1:T(8,128)S(1)} %bitcast.502), channel_id=1, source_target_pairs={{4,0},{8,4},{12,8},{16,12},{20,16},{24,20},{28,24},{0,28},{5,1},{9... | collective-permute-start | bytes 1179656 | tf_op jit(solution)/shard_map/ppermute | solution.py:16
  519.6 33.6 %collective-permute-start.13 = (f32[512,192]{0,1:T(8,128)S(1)}, f32[512,192]{0,1:T(8,128)S(1)}, u32[]{:S(2)}, u32[]{:S(2)}) collective-permute-start(f32[512,192]{0,1:T(8,128)S(1)} %bitcast.500), channel_id=1, source_target_pairs={{8,0},{12,4},{16,8},{20,12},{24,16},{28,20},{0,24},{4,28},{9,1},{1... | collective-permute-start | bytes 1179656 | tf_op jit(solution)/shard_map/ppermute | solution.py:16
  520.2 41.4 %collective-permute-start.14 = (f32[512,192]{0,1:T(8,128)S(1)}, f32[512,192]{0,1:T(8,128)S(1)}, u32[]{:S(2)}, u32[]{:S(2)}) collective-permute-start(f32[512,192]{0,1:T(8,128)S(1)} %bitcast.498), channel_id=1, source_target_pairs={{12,0},{16,4},{20,8},{24,12},{28,16},{0,20},{4,24},{8,28},{13,1},{... | collective-permute-start | bytes 1179656 | tf_op jit(solution)/shard_map/ppermute | solution.py:16
  525.8 36.2 %copy-start.38 = (bf16[2,1536,192]{1,2,0:T(8,128)(2,1)S(1)}, bf16[2,1536,192]{1,2,0:T(8,128)(2,1)}, u32[]{:S(2)}) copy-start(bf16[2,1536,192]{1,2,0:T(8,128)(2,1)} %param.17) | copy-start | bytes 3538948
  544.8 24.0 %collective-permute-start.17 = (f32[512,192]{0,1:T(8,128)S(1)}, f32[512,192]{0,1:T(8,128)S(1)}, u32[]{:S(2)}, u32[]{:S(2)}) collective-permute-start(f32[512,192]{0,1:T(8,128)S(1)} %bitcast.493), channel_id=1, source_target_pairs={{12,0},{16,4},{20,8},{24,12},{28,16},{0,20},{4,24},{8,28},{13,1},{... | collective-permute-start | bytes 1179656 | tf_op jit(solution)/shard_map/ppermute | solution.py:16
  571.9 175.2 %all-reduce.23.cloned.1.call-start = ((), (), s32[]{:S(2)}) async-start(), calls=%async_computation.12 | async-start | bytes 6291456 | tf_op jit(solution)/shard_map/psum | solution.py:193
  663.3 9.6 slice-start.2
  663.3 11.5 slice-start.8
  678.4 340.1 %all-reduce.25.cloned.1.call-start = ((), (), s32[]{:S(2)}) async-start(), calls=%async_computation.20 | async-start | bytes 12582912 | tf_op jit(solution)/shard_map/psum | solution.py:138
  678.5 68.7 %copy-start.82 = (f32[512]{0:T(512)S(1)}, f32[512]{0:T(512)}, u32[]{:S(2)}) copy-start(f32[512]{0:T(512)} %copy-done.81) | copy-start | bytes 6148
  754.7 9.7 copy-start.42
  820.8 11.5 copy-start.36
  822.6 48.6 %collective-permute-start.21 = (f32[512,192]{0,1:T(8,128)S(1)}, f32[512,192]{0,1:T(8,128)S(1)}, u32[]{:S(2)}, u32[]{:S(2)}) collective-permute-start(f32[512,192]{0,1:T(8,128)S(1)} %bitcast.496), channel_id=1, source_target_pairs={{4,0},{8,4},{12,8},{16,12},{20,16},{24,20},{28,24},{0,28},{5,1},{9... | collective-permute-start | bytes 1179656 | tf_op jit(solution)/shard_map/ppermute | solution.py:16
  826.9 44.4 %collective-permute-start.22 = (f32[512,192]{0,1:T(8,128)S(1)}, f32[512,192]{0,1:T(8,128)S(1)}, u32[]{:S(2)}, u32[]{:S(2)}) collective-permute-start(f32[512,192]{0,1:T(8,128)S(1)} %bitcast.494), channel_id=1, source_target_pairs={{8,0},{12,4},{16,8},{20,12},{24,16},{28,20},{0,24},{4,28},{9,1},{1... | collective-permute-start | bytes 1179656 | tf_op jit(solution)/shard_map/ppermute | solution.py:16
  827.6 25.7 %collective-permute-start.18 = (f32[512,192]{0,1:T(8,128)S(1)}, f32[512,192]{0,1:T(8,128)S(1)}, u32[]{:S(2)}, u32[]{:S(2)}) collective-permute-start(f32[512,192]{0,1:T(8,128)S(1)} %bitcast.503), channel_id=1, source_target_pairs={{4,0},{8,4},{12,8},{16,12},{20,16},{24,20},{28,24},{0,28},{5,1},{9... | collective-permute-start | bytes 1179656 | tf_op jit(solution)/shard_map/ppermute | solution.py:16
  828.2 33.6 %collective-permute-start.19 = (f32[512,192]{0,1:T(8,128)S(1)}, f32[512,192]{0,1:T(8,128)S(1)}, u32[]{:S(2)}, u32[]{:S(2)}) collective-permute-start(f32[512,192]{0,1:T(8,128)S(1)} %bitcast.501), channel_id=1, source_target_pairs={{8,0},{12,4},{16,8},{20,12},{24,16},{28,20},{0,24},{4,28},{9,1},{1... | collective-permute-start | bytes 1179656 | tf_op jit(solution)/shard_map/ppermute | solution.py:16
  828.8 41.4 %collective-permute-start.20 = (f32[512,192]{0,1:T(8,128)S(1)}, f32[512,192]{0,1:T(8,128)S(1)}, u32[]{:S(2)}, u32[]{:S(2)}) collective-permute-start(f32[512,192]{0,1:T(8,128)S(1)} %bitcast.499), channel_id=1, source_target_pairs={{12,0},{16,4},{20,8},{24,12},{28,16},{0,20},{4,24},{8,28},{13,1},{... | collective-permute-start | bytes 1179656 | tf_op jit(solution)/shard_map/ppermute | solution.py:16
  834.4 36.2 %copy-start.39 = (bf16[2,1536,192]{1,2,0:T(8,128)(2,1)S(1)}, bf16[2,1536,192]{1,2,0:T(8,128)(2,1)}, u32[]{:S(2)}) copy-start(bf16[2,1536,192]{1,2,0:T(8,128)(2,1)} %param.17) | copy-start | bytes 3538948
  853.4 24.0 %collective-permute-start.23 = (f32[512,192]{0,1:T(8,128)S(1)}, f32[512,192]{0,1:T(8,128)S(1)}, u32[]{:S(2)}, u32[]{:S(2)}) collective-permute-start(f32[512,192]{0,1:T(8,128)S(1)} %bitcast.492), channel_id=1, source_target_pairs={{12,0},{16,4},{20,8},{24,12},{28,16},{0,20},{4,24},{8,28},{13,1},{... | collective-permute-start | bytes 1179656 | tf_op jit(solution)/shard_map/ppermute | solution.py:16
  880.5 204.7 %reduce-scatter.24.cloned.1.call-start = ((), (), s32[]{:S(2)}) async-start(), calls=%async_computation.17 | async-start | bytes 442368
  884.2 266.5 %reduce-scatter.28.cloned.1.call-start = ((), (), s32[]{:S(2)}) async-start(), calls=%async_computation.19 | async-start | bytes 1327104
  887.9 9.5 copy-start.51
  897.3 320.3 %reduce-scatter.26.cloned.1.call-start = ((), (), s32[]{:S(2)}) async-start(), calls=%async_computation.18 | async-start | bytes 1327104
  905.8 376.0 %reduce-scatter.22.cloned.1.call-start = ((), (), s32[]{:S(2)}) async-start(), calls=%async_computation.16 | async-start | bytes 442368
  907.7 110.8 %copy-start.3 = (f32[512,1536]{1,0:T(8,128)S(1)}, f32[512,1536]{1,0:T(8,128)}, u32[]{:S(2)}) copy-start(f32[512,1536]{1,0:T(8,128)} %param.12) | copy-start | bytes 9437188
  907.7 110.8 %copy-start.73 = (f32[1536]{0:T(1024)S(1)}, f32[1536]{0:T(1024)}, u32[]{:S(2)}) copy-start(f32[1536]{0:T(1024)} %copy-done.72) | copy-start | bytes 18436
  907.7 110.8 %copy-start.80 = (f32[512]{0:T(512)S(1)}, f32[512]{0:T(512)}, u32[]{:S(2)}) copy-start(f32[512]{0:T(512)} %copy-done.79) | copy-start | bytes 6148
  1022.2 331.0 %reduce-scatter.16.cloned.1.call-start = ((), (), s32[]{:S(2)}) async-start(), calls=%async_computation.13 | async-start | bytes 2654208 | tf_op jit(solution)/shard_map/reduce_scatter | solution.py:327
  1025.6 608.2 %all-reduce.27.cloned.1.call-start = ((), (), s32[]{:S(2)}) async-start(), calls=%async_computation.21 | async-start | bytes 17301504
  1037.8 16.4 copy-start.47
  1065.5 689.1 %reduce-scatter.20.cloned.1.call-start = ((), (), s32[]{:S(2)}) async-start(), calls=%async_computation.15 | async-start | bytes 7077888 | tf_op jit(solution)/shard_map/reduce_scatter | solution.py:342
  1074.3 801.3 %reduce-scatter.18.cloned.1.call-start = ((), (), s32[]{:S(2)}) async-start(), calls=%async_computation.14 | async-start | bytes 7077888 | tf_op jit(solution)/shard_map/reduce_scatter | solution.py:339
  (101 other events, 405.7 us)
Sparse Core Ops, SparseCore 0:
  71.1 65.7 all-reduce.12
  153.0 68.5 all-reduce.14
  278.9 64.9 all-reduce.16
  365.1 68.5 all-reduce.18
  572.0 86.5 all-reduce.20
  678.5 68.5 all-reduce.22
  880.6 137.8 all-reduce.24
  1022.4 61.5 reduce-scatter.23
  1087.4 63.2 reduce-scatter.27
  1154.5 63.0 reduce-scatter.25
  1221.4 60.3 reduce-scatter.21
  1285.1 68.0 reduce-scatter.15
  1357.2 276.5 all-reduce.26
  1637.7 116.9 reduce-scatter.19
  1758.5 117.0 reduce-scatter.17
where the time goes:
time: 1890 us; the launch traced here: 1880 us
  waiting for transfers between devices  1400 us (74%)
  matrix products  249 us (13%)
  other arithmetic  89 us (5%)
  local copies, waits for them, and re-layouts  81.4 us (4%)
  starting transfers between devices  45.7 us (2%)
    unnamed x20, waiting for transfers between devices  462 us
    psum x2, waiting for transfers between devices, forward_layer(): result = middle + lax.psum(unit_part, 'tensor')  171 us
    psum x2, waiting for transfers between devices, backward_layer(): mlp_norm_grad = lax.psum(unit_back, 'tensor')  132 us
    psum x2, waiting for transfers between devices, forward_layer(): middle = residual_stream + lax.psum(head_part, 'tensor')  129 us
    reduce_scatter x1, waiting for transfers between devices, shards(): lax.psum_scatter(stacked[6].astype(jnp.bfloat16), 'dp', scatter_dimension...  119 us
    ppermute x24, waiting for transfers between devices, passed_along(): return lax.ppermute(block, axis, route)  118 us
    reduce_scatter x1, waiting for transfers between devices, shards(): lax.psum_scatter(stacked[7].astype(jnp.bfloat16), 'dp', scatter_dimension...  116 us
    psum x1, waiting for transfers between devices, backward_layer(): attn_norm_grad = lax.psum(head_back, 'tensor')  86.6 us
  transfers between devices with their start and end apart: 39, of which 25 were waited for; matrix products, arithmetic and copies ran while one was open for 9% of the time, Pallas kernels for 0%

commit v1 on v0

--- a/solution.py
+++ b/solution.py
@@ -135,7 +135,7 @@
     up_values = jnp.dot(normed_mlp, up_w, preferred_element_type=jnp.float32)
     activated = (jax.nn.silu(gate_pre) * up_values).astype(jnp.bfloat16)
     unit_part = jnp.dot(activated, down_w, preferred_element_type=jnp.float32)
-    result = middle + lax.psum(unit_part, "tensor")
+    result = middle + jnp.sum(lax.all_gather(unit_part, "tensor"), axis=0)
     record = (
         residual_stream,
         inv_attn,

time: 1890 us -> 1960 us (1.037)
  waiting for transfers between devices: 1400 us -> 1440 us
    psum x2 -> x0, waiting for transfers between devices: 171 us -> none  [forward_layer(): result = middle + lax.psum(unit_part, 'tensor')]
    all_gather x0 -> x2, waiting for transfers between devices: none -> 159 us  [forward_layer(): result = middle + jnp.sum(lax.all_gather(unit_part, 'tensor'), axis=0)]
    psum x1 -> x2, waiting for transfers between devices: 86.6 us -> 164 us  [backward_layer(): attn_norm_grad = lax.psum(head_back, 'tensor')]
    unnamed x20 -> x21, waiting for transfers between devices: 462 us -> 436 us
    unnamed x269 -> x253, local copies, waits for them, and re-layouts: 43.1 us -> 45.5 us
  transfers between devices with their start and end apart: 39 -> 40, of which waited for: 25 -> 26; matrix products, arithmetic and copies ran while one was open for 9% -> 9% of each run, Pallas kernels for 0% -> 0%
where the time goes in v1:
time: 1960 us; the launch traced here: 1950 us
  waiting for transfers between devices  1440 us (73%)
  matrix products  251 us (13%)
  other arithmetic  107 us (5%)
  local copies, waits for them, and re-layouts  85.2 us (4%)
  starting transfers between devices  46.2 us (2%)
    unnamed x21, waiting for transfers between devices  436 us
    psum x2, waiting for transfers between devices, backward_layer(): attn_norm_grad = lax.psum(head_back, 'tensor')  164 us
    all_gather x2, waiting for transfers between devices, forward_layer(): result = middle + jnp.sum(lax.all_gather(unit_part, 'tensor'), axis=0)  159 us
    psum x2, waiting for transfers between devices, backward_layer(): mlp_norm_grad = lax.psum(unit_back, 'tensor')  132 us
    psum x2, waiting for transfers between devices, forward_layer(): middle = residual_stream + lax.psum(head_part, 'tensor')  129 us
    reduce_scatter x1, waiting for transfers between devices, shards(): lax.psum_scatter(stacked[6].astype(jnp.bfloat16), 'dp', scatter_dimension...  119 us
    ppermute x24, waiting for transfers between devices, passed_along(): return lax.ppermute(block, axis, route)  118 us
    reduce_scatter x1, waiting for transfers between devices, shards(): lax.psum_scatter(stacked[7].astype(jnp.bfloat16), 'dp', scatter_dimension...  115 us
  transfers between devices with their start and end apart: 40, of which 26 were waited for; matrix products, arithmetic and copies ran while one was open for 9% of the time, Pallas kernels for 0%

profile of v1, /device:TPU:0, one launch (start us, length us, event | category | flops | bytes accessed | tf_op | source)
XLA Modules:
  0.0 1946.8 jit_solution(11635481319433784794)
XLA Ops:
  38.5 14.9 collective-permute-done.5
  53.4 4.6 fusion.10
  58.0 3.6 exponential_reduce_fusion.1
  63.8 4.4 convolution_convert_fusion.15
  72.3 64.6 %all-reduce.11.cloned.1.call-done = f32[512,1536]{1,0:T(8,128)} async-done(((f32[512,1536]{1,0:T(8,128)}), f32[512,1536]{1,0:T(8,128)}) %all-reduce.11.cloned.1.call-update) | async-done | bytes 3145744 | tf_op jit(solution)/shard_map/psum | solution.py:131
  140.6 4.5 fusion.38
  149.5 3.5 fusion.31
  155.4 79.9 %all-gather.5.cloned.1.call-done = f32[2048,1536]{1,0:T(8,128)} async-done(((f32[512,1536]{1,0:T(8,128)}), f32[2048,1536]{1,0:T(8,128)}) %all-gather.5.cloned.1.call-update) | async-done | bytes 12582928 | tf_op jit(solution)/shard_map/all_gather | solution.py:138
  235.4 8.0 reduce_sum.195
  260.3 22.9 %collective-permute-done.11 = bf16[512,192]{0,1:T(8,128)(2,1)S(1)} collective-permute-done((bf16[512,192]{0,1:T(8,128)(2,1)S(1)}, bf16[512,192]{0,1:T(8,128)(2,1)S(1)}, u32[]{:S(2)}, u32[]{:S(2)}) %collective-permute-start.11) | collective-permute-done | bytes 196640 | tf_op jit(solution)/shard_map/ppermute | solution.py:16
  286.4 3.6 exponential_reduce_fusion
  292.1 4.4 convolution_convert_fusion.14
  297.2 3.9 fusion.77
  301.4 64.5 %all-reduce.13.cloned.1.call-done = f32[512,1536]{1,0:T(8,128)} async-done(((f32[512,1536]{1,0:T(8,128)}), f32[512,1536]{1,0:T(8,128)}) %all-reduce.13.cloned.1.call-update) | async-done | bytes 3145744 | tf_op jit(solution)/shard_map/psum | solution.py:131
  369.7 5.6 fusion.23
  377.9 3.7 multiply_convert_fusion.6
  383.5 3.5 convolution_add_fusion.5
  387.0 5.7 fusion.20
  392.8 62.9 %all-reduce.15.cloned.1.call-done = f32[512,1536]{1,0:T(8,128)} async-done(((f32[512,1536]{1,0:T(8,128)}), f32[512,1536]{1,0:T(8,128)}) %all-reduce.15.cloned.1.call-update) | async-done | bytes 3145744 | tf_op jit(solution)/shard_map/psum | solution.py:193
  455.7 4.2 multiply_reduce_fusion
  460.5 78.8 %all-gather.7.cloned.1.call-done = f32[2048,1536]{1,0:T(8,128)} async-done(((f32[512,1536]{1,0:T(8,128)}), f32[2048,1536]{1,0:T(8,128)}) %all-gather.7.cloned.1.call-update) | async-done | bytes 12582928 | tf_op jit(solution)/shard_map/all_gather | solution.py:138
  539.3 8.0 reduce_sum.199
  547.3 7.4 multiply_add_fusion.3
  557.3 9.6 convolution_bitcast_fusion.1
  566.8 8.2 fusion.188
  575.0 25.2 %fusion.63 = f32[2048,2,96]{0,2,1:T(8,128)} fusion(bf16[512,2,2,96]{0,3,2,1:T(8,128)(2,1)} %bitcast.495, f32[2,2048,512,2]{2,1,3,0:T(8,128)} %fusion.188, f32[2,2048,512,2]{2,1,3,0:T(8,128)} %copy-done.10, f32[2,2,512]{2,1,0:T(2,128)S(1)} %copy-done.87, pred[512,2048]{0,1:T(8,128)(4,1)} %copy-done.20), kind=kOutput, calls=%fused_computation.113 | convolution fusion | flops 851447808 | bytes 36577280 | tf_op jit(solution)/shard_map/kgqt,qkgd->tkd/dot_general | solution.py:83
  600.3 25.0 %fusion.41 = f32[2,96,2,512]{3,1,2,0:T(8,128)} fusion(f32[2,2048,512,2]{2,1,3,0:T(8,128)} %fusion.188, f32[2,2048,512,2]{2,1,3,0:T(8,128)} %copy-done.10, f32[2,2,512]{2,1,0:T(2,128)S(1)} %copy-done.87, pred[512,2048]{0,1:T(8,128)(4,1)} %copy-done.20, bf16[512,2,96]{0,2,1:T(8,128)(2,1)} %bitcast.534, bf16[512,2,96]{0,2,1:T(8,128)(2,1)} %bitcast.532, ...), kind=kOutput, calls=%fused_computation.87 | convolution fusion | flops 854593536 | bytes 36184064 | tf_op jit(solution)/shard_map/kgqt,tkd->qkgd/dot_general | solution.py:80
  627.0 4.3 collective-permute-start.15
  638.7 18.9 collective-permute-done.12
  660.4 5.6 collective-permute-done.13
  666.0 8.4 collective-permute-done.14
  675.5 6.7 collective-permute-done.17
  685.4 86.3 %all-reduce.17.cloned.1.call-done = f32[512,1536]{1,0:T(8,128)} async-done(((f32[512,1536]{1,0:T(8,128)}), f32[512,1536]{1,0:T(8,128)}) %all-reduce.17.cloned.1.call-update) | async-done | bytes 3145744 | tf_op jit(solution)/shard_map/psum | solution.py:229
  771.7 4.3 multiply_reduce_fusion.2
  780.0 5.1 multiply_convert_fusion.4
  787.0 5.4 convolution_add_fusion.4
  792.5 68.6 %all-reduce.19.cloned.1.call-done = f32[512,1536]{1,0:T(8,128)} async-done(((f32[512,1536]{1,0:T(8,128)}), f32[512,1536]{1,0:T(8,128)}) %all-reduce.19.cloned.1.call-update) | async-done | bytes 3145744 | tf_op jit(solution)/shard_map/psum | solution.py:193
  868.7 9.5 convolution_bitcast_fusion
  878.2 8.1 fusion.189
  886.3 24.6 %fusion.62 = f32[2048,2,96]{0,2,1:T(8,128)} fusion(bf16[512,2,2,96]{0,3,2,1:T(8,128)(2,1)S(1)} %bitcast.493, f32[2,2048,512,2]{2,1,3,0:T(8,128)} %fusion.189, f32[2,2048,512,2]{2,1,3,0:T(8,128)} %copy-done.9, f32[2,2,512]{2,1,0:T(2,128)S(1)} %copy-done.85, pred[512,2048]{0,1:T(8,128)(4,1)S(1)} %copy-done.23), kind=kOutput, calls=%fused_computation.112 | convolution fusion | flops 851447808 | bytes 36577280 | tf_op jit(solution)/shard_map/kgqt,qkgd->tkd/dot_general | solution.py:83
  911.0 23.6 %fusion.44 = f32[2,96,2,512]{3,1,2,0:T(8,128)S(1)} fusion(f32[2,2048,512,2]{2,1,3,0:T(8,128)} %fusion.189, f32[2,2048,512,2]{2,1,3,0:T(8,128)} %copy-done.9, f32[2,2,512]{2,1,0:T(2,128)S(1)} %copy-done.85, pred[512,2048]{0,1:T(8,128)(4,1)S(1)} %copy-done.23, bf16[512,2,96]{0,2,1:T(8,128)(2,1)} %bitcast.14, bf16[512,2,96]{0,2,1:T(8,128)(2,1)} %bitcast.13, ...), kind=kOutput, calls=%fused_computation.90 | convolution fusion | flops 854593536 | bytes 36184064 | tf_op jit(solution)/shard_map/kgqt,tkd->qkgd/dot_general | solution.py:80
  936.5 4.3 collective-permute-start.21
  948.2 19.0 collective-permute-done.18
  969.8 5.8 collective-permute-done.19
  975.6 8.4 collective-permute-done.20
  985.1 6.1 collective-permute-done.23
  1003.3 77.7 %all-reduce.21.cloned.1.call-done = f32[512,1536]{1,0:T(8,128)} async-done(((f32[512,1536]{1,0:T(8,128)}), f32[512,1536]{1,0:T(8,128)}) %all-reduce.21.cloned.1.call-update) | async-done | bytes 3145744 | tf_op jit(solution)/shard_map/psum | solution.py:229
  1087.1 4.9 copy.91
  1091.9 4.5 reshape.442
  1101.5 4.8 copy.89
  1106.4 4.5 reshape.440
  1117.6 4.2 fusion.17
  1129.6 16.5 copy.64
  1150.4 6.9 copy.63
  1157.4 3.7 fusion.15
  1166.3 3.7 fusion.13
  1178.5 5.2 multiply_add_fusion
  1183.7 26.8 %reduce-scatter.22.cloned.1.call-done = bf16[192,2]{1,0:T(8,128)(2,1)} async-done(((bf16[1536,2]{1,0:T(8,128)(2,1)}), bf16[192,2]{1,0:T(8,128)(2,1)}) %reduce-scatter.22.cloned.1.call-update) | async-done | bytes 784
  1212.0 65.1 %reduce-scatter.28.cloned.1.call-done = bf16[192,384]{1,0:T(8,128)(2,1)} async-done(((bf16[1536,384]{1,0:T(8,128)(2,1)}), bf16[192,384]{1,0:T(8,128)(2,1)}) %reduce-scatter.28.cloned.1.call-update) | async-done | bytes 147472
  1279.2 64.7 %reduce-scatter.26.cloned.1.call-done = bf16[192,384]{1,0:T(8,128)(2,1)} async-done(((bf16[1536,384]{1,0:T(8,128)(2,1)}), bf16[192,384]{1,0:T(8,128)(2,1)}) %reduce-scatter.26.cloned.1.call-update) | async-done | bytes 147472
  1346.1 69.4 %reduce-scatter.16.cloned.1.call-done = bf16[2,192,384]{2,1,0:T(8,128)(2,1)} async-done(((bf16[2,1536,384]{2,1,0:T(8,128)(2,1)}), bf16[2,192,384]{2,1,0:T(8,128)(2,1)}) %reduce-scatter.16.cloned.1.call-update) | async-done | bytes 294928 | tf_op jit(solution)/shard_map/reduce_scatter | solution.py:327
  1417.3 278.6 %all-reduce.23.cloned.1.call-done = (bf16[2,384,1536]{1,0,2:T(2,128)(2,1)}, bf16[2,1024,1536]{1,0,2:T(2,128)(2,1)}) async-done(((bf16[2,384,1536]{1,0,2:T(2,128)(2,1)}, bf16[2,1024,1536]{1,0,2:T(2,128)(2,1)}), (bf16[2,384,1536]{1,0,2:T(2,128)(2,1)}, bf16[2,1024,1536]{1,0,2:T(2,128)(2,1)})) %all-reduce.23.cloned.1.call-update) | async-done | bytes 8650768
  1701.2 115.5 %reduce-scatter.20.cloned.1.call-done = bf16[2,192,1024]{2,1,0:T(8,128)(2,1)} async-done(((bf16[2,1536,1024]{2,1,0:T(8,128)(2,1)}), bf16[2,192,1024]{2,1,0:T(8,128)(2,1)}) %reduce-scatter.20.cloned.1.call-update) | async-done | bytes 786448 | tf_op jit(solution)/shard_map/reduce_scatter | solution.py:342
  1819.1 118.5 %reduce-scatter.18.cloned.1.call-done = bf16[2,192,1024]{2,1,0:T(8,128)(2,1)} async-done(((bf16[2,1536,1024]{2,1,0:T(8,128)(2,1)}), bf16[2,192,1024]{2,1,0:T(8,128)(2,1)}) %reduce-scatter.18.cloned.1.call-update) | async-done | bytes 786448 | tf_op jit(solution)/shard_map/reduce_scatter | solution.py:339
  (451 shorter events, 196.8 us)
Async XLA Ops:
  7.2 129.7 %all-reduce.11.cloned.1.call-start = ((), (), s32[]{:S(2)}) async-start(), calls=%async_computation.7 | async-start | bytes 6291456 | tf_op jit(solution)/shard_map/psum | solution.py:131
  16.0 10.4 copy-start.71
  16.8 19.0 collective-permute-start.3
  19.7 18.7 collective-permute-start.4
  21.3 32.0 %collective-permute-start.5 = (bf16[512,192]{0,1:T(8,128)(2,1)}, bf16[512,192]{0,1:T(8,128)(2,1)}, u32[]{:S(2)}, u32[]{:S(2)}) collective-permute-start(bf16[512,192]{0,1:T(8,128)(2,1)} %bitcast.11), channel_id=1, source_target_pairs={{20,0},{24,4},{28,8},{0,12},{4,16},{8,20},{12,24},{16,28},{21,1},{... | collective-permute-start | bytes 589832 | tf_op jit(solution)/shard_map/ppermute | solution.py:16
  24.6 37.1 %collective-permute-start = (bf16[512,192]{0,1:T(8,128)(2,1)S(1)}, bf16[512,192]{0,1:T(8,128)(2,1)S(1)}, u32[]{:S(2)}, u32[]{:S(2)}) collective-permute-start(bf16[512,192]{0,1:T(8,128)(2,1)S(1)} %convolution_convert_fusion.19), channel_id=1, source_target_pairs={{28,0},{0,4},{4,8},{8,12},{12,16},{16,20},{20,24},{24,28},{29,1},{... | collective-permute-start | bytes 589832 | tf_op jit(solution)/shard_map/ppermute | solution.py:16
  26.1 35.6 %collective-permute-start.1 = (bf16[512,192]{0,1:T(8,128)(2,1)S(1)}, bf16[512,192]{0,1:T(8,128)(2,1)}, u32[]{:S(2)}, u32[]{:S(2)}) collective-permute-start(bf16[512,192]{0,1:T(8,128)(2,1)S(1)} %convolution_convert_fusion.19), channel_id=1, source_target_pairs={{24,0},{28,4},{0,8},{4,12},{8,16},{12,20},{16,24},{20,28},{25,1},{... | collective-permute-start | bytes 589832 | tf_op jit(solution)/shard_map/ppermute | solution.py:16
  35.6 27.4 %copy-start.20 = (pred[512,2048]{0,1:T(8,128)(4,1)}, pred[512,2048]{0,1:T(8,128)(4,1)S(1)}, u32[]{:S(2)}) copy-start(pred[512,2048]{0,1:T(8,128)(4,1)S(1)} %compare_and_fusion) | copy-start | bytes 3145732
  35.8 22.2 %copy-start.61 = (bf16[512,4,96]{0,2,1:T(8,128)(2,1)}, bf16[512,4,96]{0,2,1:T(8,128)(2,1)S(1)}, u32[]{:S(2)}) copy-start(bf16[512,4,96]{0,2,1:T(8,128)(2,1)S(1)} %fusion.97) | copy-start | bytes 1179652
  35.8 25.9 %collective-permute-start.2 = (bf16[512,192]{0,1:T(8,128)(2,1)S(1)}, bf16[512,192]{0,1:T(8,128)(2,1)S(1)}, u32[]{:S(2)}, u32[]{:S(2)}) collective-permute-start(bf16[512,192]{0,1:T(8,128)(2,1)S(1)} %convolution_convert_fusion.19), channel_id=1, source_target_pairs={{20,0},{24,4},{28,8},{0,12},{4,16},{8,20},{12,24},{16,28},{21,1},{... | collective-permute-start | bytes 589832 | tf_op jit(solution)/shard_map/ppermute | solution.py:16
  71.0 164.4 %all-gather.5.cloned.1.call-start = ((), (), s32[]{:S(2)}) async-start(), calls=%async_computation.16 | async-start | bytes 15728640 | tf_op jit(solution)/shard_map/all_gather | solution.py:138
  72.3 68.0 %copy-start.67 = (f32[1536]{0:T(1024)}, f32[1536]{0:T(1024)S(1)}, u32[]{:S(2)}) copy-start(f32[1536]{0:T(1024)S(1)} %get-tuple-element.53) | copy-start | bytes 18436
  153.0 212.9 %all-reduce.13.cloned.1.call-start = ((), (), s32[]{:S(2)}) async-start(), calls=%async_computation.8 | async-start | bytes 6291456 | tf_op jit(solution)/shard_map/psum | solution.py:131
  246.1 10.1 copy-start.14
  248.1 35.2 %copy-start.64 = (bf16[512,2,96]{0,2,1:T(8,128)(2,1)}, bf16[512,2,96]{0,2,1:T(8,128)(2,1)S(1)}, u32[]{:S(2)}) copy-start(bf16[512,2,96]{0,2,1:T(8,128)(2,1)S(1)} %fusion.129) | copy-start | bytes 589828
  248.1 10.6 collective-permute-start.9
  249.6 10.7 collective-permute-start.10
  251.1 32.2 %collective-permute-start.11 = (bf16[512,192]{0,1:T(8,128)(2,1)S(1)}, bf16[512,192]{0,1:T(8,128)(2,1)S(1)}, u32[]{:S(2)}, u32[]{:S(2)}) collective-permute-start(bf16[512,192]{0,1:T(8,128)(2,1)S(1)} %bitcast.510), channel_id=1, source_target_pairs={{20,0},{24,4},{28,8},{0,12},{4,16},{8,20},{12,24},{16,28},{21,1},{... | collective-permute-start | bytes 589832 | tf_op jit(solution)/shard_map/ppermute | solution.py:16
  254.2 35.9 %collective-permute-start.6 = (bf16[512,192]{0,1:T(8,128)(2,1)S(1)}, bf16[512,192]{0,1:T(8,128)(2,1)S(1)}, u32[]{:S(2)}, u32[]{:S(2)}) collective-permute-start(bf16[512,192]{0,1:T(8,128)(2,1)S(1)} %convolution_convert_fusion.18), channel_id=1, source_target_pairs={{28,0},{0,4},{4,8},{8,12},{12,16},{16,20},{20,24},{24,28},{29,1},{... | collective-permute-start | bytes 589832 | tf_op jit(solution)/shard_map/ppermute | solution.py:16
  255.7 34.4 %collective-permute-start.7 = (bf16[512,192]{0,1:T(8,128)(2,1)S(1)}, bf16[512,192]{0,1:T(8,128)(2,1)S(1)}, u32[]{:S(2)}, u32[]{:S(2)}) collective-permute-start(bf16[512,192]{0,1:T(8,128)(2,1)S(1)} %convolution_convert_fusion.18), channel_id=1, source_target_pairs={{24,0},{28,4},{0,8},{4,12},{8,16},{12,20},{16,24},{20,28},{25,1},{... | collective-permute-start | bytes 589832 | tf_op jit(solution)/shard_map/ppermute | solution.py:16
  257.0 26.3 %copy-start.21 = (pred[512,2048]{0,1:T(8,128)(4,1)S(1)}, pred[512,2048]{0,1:T(8,128)(4,1)}, u32[]{:S(2)}) copy-start(pred[512,2048]{0,1:T(8,128)(4,1)} %copy-done.20) | copy-start | bytes 3145732
  257.3 29.0 %copy-start.63 = (bf16[512,4,96]{0,2,1:T(8,128)(2,1)}, bf16[512,4,96]{0,2,1:T(8,128)(2,1)S(1)}, u32[]{:S(2)}) copy-start(bf16[512,4,96]{0,2,1:T(8,128)(2,1)S(1)} %fusion.99) | copy-start | bytes 1179652
  258.7 27.7 %copy-start.90 = (bf16[512,192]{0,1:T(8,128)(2,1)}, bf16[512,192]{0,1:T(8,128)(2,1)S(1)}, u32[]{:S(2)}) copy-start(bf16[512,192]{0,1:T(8,128)(2,1)S(1)} %collective-permute-done.9) | copy-start | bytes 589828
  258.7 31.4 %collective-permute-start.8 = (bf16[512,192]{0,1:T(8,128)(2,1)S(1)}, bf16[512,192]{0,1:T(8,128)(2,1)S(1)}, u32[]{:S(2)}, u32[]{:S(2)}) collective-permute-start(bf16[512,192]{0,1:T(8,128)(2,1)S(1)} %convolution_convert_fusion.18), channel_id=1, source_target_pairs={{20,0},{24,4},{28,8},{0,12},{4,16},{8,20},{12,24},{16,28},{21,1},{... | collective-permute-start | bytes 589832 | tf_op jit(solution)/shard_map/ppermute | solution.py:16
  260.3 26.0 %copy-start.91 = (bf16[512,192]{0,1:T(8,128)(2,1)}, bf16[512,192]{0,1:T(8,128)(2,1)S(1)}, u32[]{:S(2)}) copy-start(bf16[512,192]{0,1:T(8,128)(2,1)S(1)} %collective-permute-done.10) | copy-start | bytes 589828
  301.2 68.1 %copy-start.69 = (f32[1536]{0:T(1024)S(1)}, f32[1536]{0:T(1024)}, u32[]{:S(2)}) copy-start(f32[1536]{0:T(1024)} %get-tuple-element.52) | copy-start | bytes 18436
  301.2 154.5 %all-reduce.15.cloned.1.call-start = ((), (), s32[]{:S(2)}) async-start(), calls=%async_computation.9 | async-start | bytes 6291456 | tf_op jit(solution)/shard_map/psum | solution.py:193
  387.0 152.3 %all-gather.7.cloned.1.call-start = ((), (), s32[]{:S(2)}) async-start(), calls=%async_computation.17 | async-start | bytes 15728640 | tf_op jit(solution)/shard_map/all_gather | solution.py:138
  392.7 379.0 %all-reduce.17.cloned.1.call-start = ((), (), s32[]{:S(2)}) async-start(), calls=%async_computation.10 | async-start | bytes 6291456 | tf_op jit(solution)/shard_map/psum | solution.py:229
  557.3 9.6 copy-start.37
  625.3 11.1 copy-start.29
  627.0 48.6 %collective-permute-start.15 = (f32[512,192]{0,1:T(8,128)S(1)}, f32[512,192]{0,1:T(8,128)S(1)}, u32[]{:S(2)}, u32[]{:S(2)}) collective-permute-start(f32[512,192]{0,1:T(8,128)S(1)} %bitcast.501), channel_id=1, source_target_pairs={{4,0},{8,4},{12,8},{16,12},{20,16},{24,20},{28,24},{0,28},{5,1},{9... | collective-permute-start | bytes 1179656 | tf_op jit(solution)/shard_map/ppermute | solution.py:16
  631.3 44.3 %collective-permute-start.16 = (f32[512,192]{0,1:T(8,128)S(1)}, f32[512,192]{0,1:T(8,128)S(1)}, u32[]{:S(2)}, u32[]{:S(2)}) collective-permute-start(f32[512,192]{0,1:T(8,128)S(1)} %bitcast.499), channel_id=1, source_target_pairs={{8,0},{12,4},{16,8},{20,12},{24,16},{28,20},{0,24},{4,28},{9,1},{1... | collective-permute-start | bytes 1179656 | tf_op jit(solution)/shard_map/ppermute | solution.py:16
  631.9 25.7 %collective-permute-start.12 = (f32[512,192]{0,1:T(8,128)S(1)}, f32[512,192]{0,1:T(8,128)S(1)}, u32[]{:S(2)}, u32[]{:S(2)}) collective-permute-start(f32[512,192]{0,1:T(8,128)S(1)} %bitcast.506), channel_id=1, source_target_pairs={{4,0},{8,4},{12,8},{16,12},{20,16},{24,20},{28,24},{0,28},{5,1},{9... | collective-permute-start | bytes 1179656 | tf_op jit(solution)/shard_map/ppermute | solution.py:16
  632.6 33.5 %collective-permute-start.13 = (f32[512,192]{0,1:T(8,128)S(1)}, f32[512,192]{0,1:T(8,128)S(1)}, u32[]{:S(2)}, u32[]{:S(2)}) collective-permute-start(f32[512,192]{0,1:T(8,128)S(1)} %bitcast.504), channel_id=1, source_target_pairs={{8,0},{12,4},{16,8},{20,12},{24,16},{28,20},{0,24},{4,28},{9,1},{1... | collective-permute-start | bytes 1179656 | tf_op jit(solution)/shard_map/ppermute | solution.py:16
  633.1 41.4 %collective-permute-start.14 = (f32[512,192]{0,1:T(8,128)S(1)}, f32[512,192]{0,1:T(8,128)S(1)}, u32[]{:S(2)}, u32[]{:S(2)}) collective-permute-start(f32[512,192]{0,1:T(8,128)S(1)} %bitcast.502), channel_id=1, source_target_pairs={{12,0},{16,4},{20,8},{24,12},{28,16},{0,20},{4,24},{8,28},{13,1},{... | collective-permute-start | bytes 1179656 | tf_op jit(solution)/shard_map/ppermute | solution.py:16
  638.7 36.1 %copy-start.31 = (bf16[2,1536,192]{1,2,0:T(8,128)(2,1)S(1)}, bf16[2,1536,192]{1,2,0:T(8,128)(2,1)}, u32[]{:S(2)}) copy-start(bf16[2,1536,192]{1,2,0:T(8,128)(2,1)} %param.17) | copy-start | bytes 3538948
  657.6 24.6 %collective-permute-start.17 = (f32[512,192]{0,1:T(8,128)S(1)}, f32[512,192]{0,1:T(8,128)S(1)}, u32[]{:S(2)}, u32[]{:S(2)}) collective-permute-start(f32[512,192]{0,1:T(8,128)S(1)} %bitcast.497), channel_id=1, source_target_pairs={{12,0},{16,4},{20,8},{24,12},{28,16},{0,20},{4,24},{8,28},{13,1},{... | collective-permute-start | bytes 1179656 | tf_op jit(solution)/shard_map/ppermute | solution.py:16
  685.3 86.4 %copy-start.78 = (f32[512]{0:T(512)S(1)}, f32[512]{0:T(512)}, u32[]{:S(2)}) copy-start(f32[512]{0:T(512)} %copy-done.77) | copy-start | bytes 6148
  685.3 175.8 %all-reduce.19.cloned.1.call-start = ((), (), s32[]{:S(2)}) async-start(), calls=%async_computation.11 | async-start | bytes 6291456 | tf_op jit(solution)/shard_map/psum | solution.py:193
  792.4 68.7 %copy-start.68 = (f32[1536]{0:T(1024)S(1)}, f32[1536]{0:T(1024)}, u32[]{:S(2)}) copy-start(f32[1536]{0:T(1024)} %copy-done.67) | copy-start | bytes 18436
  792.4 68.7 %copy-start.76 = (f32[512]{0:T(512)S(1)}, f32[512]{0:T(512)}, u32[]{:S(2)}) copy-start(f32[512]{0:T(512)} %copy-done.75) | copy-start | bytes 6148
  792.4 288.6 %all-reduce.21.cloned.1.call-start = ((), (), s32[]{:S(2)}) async-start(), calls=%async_computation.12 | async-start | bytes 6291456 | tf_op jit(solution)/shard_map/psum | solution.py:229
  868.7 9.5 copy-start.35
  934.6 11.5 copy-start.30
  936.5 48.6 %collective-permute-start.21 = (f32[512,192]{0,1:T(8,128)S(1)}, f32[512,192]{0,1:T(8,128)S(1)}, u32[]{:S(2)}, u32[]{:S(2)}) collective-permute-start(f32[512,192]{0,1:T(8,128)S(1)} %bitcast.500), channel_id=1, source_target_pairs={{4,0},{8,4},{12,8},{16,12},{20,16},{24,20},{28,24},{0,28},{5,1},{9... | collective-permute-start | bytes 1179656 | tf_op jit(solution)/shard_map/ppermute | solution.py:16
  940.8 44.4 %collective-permute-start.22 = (f32[512,192]{0,1:T(8,128)S(1)}, f32[512,192]{0,1:T(8,128)S(1)}, u32[]{:S(2)}, u32[]{:S(2)}) collective-permute-start(f32[512,192]{0,1:T(8,128)S(1)} %bitcast.498), channel_id=1, source_target_pairs={{8,0},{12,4},{16,8},{20,12},{24,16},{28,20},{0,24},{4,28},{9,1},{1... | collective-permute-start | bytes 1179656 | tf_op jit(solution)/shard_map/ppermute | solution.py:16
  941.4 25.7 %collective-permute-start.18 = (f32[512,192]{0,1:T(8,128)S(1)}, f32[512,192]{0,1:T(8,128)S(1)}, u32[]{:S(2)}, u32[]{:S(2)}) collective-permute-start(f32[512,192]{0,1:T(8,128)S(1)} %bitcast.507), channel_id=1, source_target_pairs={{4,0},{8,4},{12,8},{16,12},{20,16},{24,20},{28,24},{0,28},{5,1},{9... | collective-permute-start | bytes 1179656 | tf_op jit(solution)/shard_map/ppermute | solution.py:16
  942.1 33.6 %collective-permute-start.19 = (f32[512,192]{0,1:T(8,128)S(1)}, f32[512,192]{0,1:T(8,128)S(1)}, u32[]{:S(2)}, u32[]{:S(2)}) collective-permute-start(f32[512,192]{0,1:T(8,128)S(1)} %bitcast.505), channel_id=1, source_target_pairs={{8,0},{12,4},{16,8},{20,12},{24,16},{28,20},{0,24},{4,28},{9,1},{1... | collective-permute-start | bytes 1179656 | tf_op jit(solution)/shard_map/ppermute | solution.py:16
  942.6 41.4 %collective-permute-start.20 = (f32[512,192]{0,1:T(8,128)S(1)}, f32[512,192]{0,1:T(8,128)S(1)}, u32[]{:S(2)}, u32[]{:S(2)}) collective-permute-start(f32[512,192]{0,1:T(8,128)S(1)} %bitcast.503), channel_id=1, source_target_pairs={{12,0},{16,4},{20,8},{24,12},{28,16},{0,20},{4,24},{8,28},{13,1},{... | collective-permute-start | bytes 1179656 | tf_op jit(solution)/shard_map/ppermute | solution.py:16
  948.2 36.2 %copy-start.32 = (bf16[2,1536,192]{1,2,0:T(8,128)(2,1)S(1)}, bf16[2,1536,192]{1,2,0:T(8,128)(2,1)}, u32[]{:S(2)}) copy-start(bf16[2,1536,192]{1,2,0:T(8,128)(2,1)} %param.17) | copy-start | bytes 3538948
  967.2 24.0 %collective-permute-start.23 = (f32[512,192]{0,1:T(8,128)S(1)}, f32[512,192]{0,1:T(8,128)S(1)}, u32[]{:S(2)}, u32[]{:S(2)}) collective-permute-start(f32[512,192]{0,1:T(8,128)S(1)} %bitcast.496), channel_id=1, source_target_pairs={{12,0},{16,4},{20,8},{24,12},{28,16},{0,20},{4,24},{8,28},{13,1},{... | collective-permute-start | bytes 1179656 | tf_op jit(solution)/shard_map/ppermute | solution.py:16
  994.3 86.7 %copy-start.3 = (f32[512,1536]{1,0:T(8,128)S(1)}, f32[512,1536]{1,0:T(8,128)}, u32[]{:S(2)}) copy-start(f32[512,1536]{1,0:T(8,128)} %param.12) | copy-start | bytes 9437188
  994.3 86.7 %copy-start.66 = (f32[1536]{0:T(1024)S(1)}, f32[1536]{0:T(1024)}, u32[]{:S(2)}) copy-start(f32[1536]{0:T(1024)} %copy-done.65) | copy-start | bytes 18436
  994.3 86.7 %copy-start.74 = (f32[512]{0:T(512)S(1)}, f32[512]{0:T(512)}, u32[]{:S(2)}) copy-start(f32[512]{0:T(512)} %copy-done.73) | copy-start | bytes 6148
  994.3 182.7 %reduce-scatter.24.cloned.1.call-start = ((), (), s32[]{:S(2)}) async-start(), calls=%async_computation.19 | async-start | bytes 442368
  1000.4 210.1 %reduce-scatter.22.cloned.1.call-start = ((), (), s32[]{:S(2)}) async-start(), calls=%async_computation.18 | async-start | bytes 442368
  1084.6 192.4 %reduce-scatter.28.cloned.1.call-start = ((), (), s32[]{:S(2)}) async-start(), calls=%async_computation.21 | async-start | bytes 1327104
  1096.4 247.5 %reduce-scatter.26.cloned.1.call-start = ((), (), s32[]{:S(2)}) async-start(), calls=%async_computation.20 | async-start | bytes 1327104
  1110.9 304.6 %reduce-scatter.16.cloned.1.call-start = ((), (), s32[]{:S(2)}) async-start(), calls=%async_computation.13 | async-start | bytes 2654208 | tf_op jit(solution)/shard_map/reduce_scatter | solution.py:327
  1117.1 578.7 %all-reduce.23.cloned.1.call-start = ((), (), s32[]{:S(2)}) async-start(), calls=%async_computation.22 | async-start | bytes 17301504
  1129.6 16.5 copy-start.40
  1157.3 659.3 %reduce-scatter.20.cloned.1.call-start = ((), (), s32[]{:S(2)}) async-start(), calls=%async_computation.15 | async-start | bytes 7077888 | tf_op jit(solution)/shard_map/reduce_scatter | solution.py:342
  1166.1 771.5 %reduce-scatter.18.cloned.1.call-start = ((), (), s32[]{:S(2)}) async-start(), calls=%async_computation.14 | async-start | bytes 7077888 | tf_op jit(solution)/shard_map/reduce_scatter | solution.py:339
  (94 other events, 392.6 us)
Sparse Core Ops, SparseCore 0:
  71.1 65.7 all-reduce.10
  153.1 82.1 all-gather.4
  301.3 64.5 all-reduce.12
  387.1 68.5 all-reduce.14
  457.1 82.1 all-gather.6
  685.5 86.1 all-reduce.16
  792.5 68.5 all-reduce.18
  994.4 86.5 all-reduce.20
  1084.8 61.5 reduce-scatter.23
  1150.1 60.4 reduce-scatter.21
  1213.9 63.1 reduce-scatter.27
  1280.9 63.0 reduce-scatter.25
  1347.4 67.9 reduce-scatter.15
  1419.3 276.4 all-reduce.22
  1699.7 116.9 reduce-scatter.19
  1820.5 117.0 reduce-scatter.17
